TPU v7x, 256 devices: a whole 4x4x8 slice. The times are simulated.
256 devices in a mesh: src: 32 (over z, y), rcv: 8 (over x, core).
Axes of the slice: x: 4, y: 4, z: 8, core: 2. Of those that a mesh axis runs over, the one named last changes fastest.
Arguments:
- field: bfloat16 [2, 16384, 4096], P(None, 'rcv', 'src'), may hold values from -6 to 6
- u_basis: bfloat16 [32, 8, 2, 8, 2, 160, 256], P('src', 'rcv'), may hold values from -0.0390625 to 0.0390625
- v_basis: bfloat16 [32, 8, 2, 8, 160, 2, 256], P('src', 'rcv'), may hold values from -0.25 to 0.25
- tile_ranks: int32 [32, 8, 2, 8], P('src', 'rcv'), may hold values from 32 to 160, as said below
- window_start: int32 [32], replicated, may hold values from 0 to 56
Outputs:
- predicted: bfloat16 [2, 2048, 4096], P(None, 'rcv', 'src')
Inputs may be any that keep to these rules, and one draw needn't show every extreme that they name: `tile_ranks`: on every device of the mesh at least one of its tiles has rank 160.
All inputs are finite; a program needn't handle non-finite values.
Results may differ from a plain program's by a relative error of at most 0.0058.
Values may be sent and summed in bfloat16 or wider, within the bound.
A program may use at most 192 MiB of HBM per device.

v0:
```python
import jax
import jax.numpy as jnp
from jax import lax
from jax.sharding import PartitionSpec as P

AR = 8


def split_up(array, dim, peers):
    before, after = (array.shape[:dim], array.shape[dim + 1 :])
    return jnp.moveaxis(array.reshape(*before, peers, -1, *after), dim, 0)


def sent_and_summed(array, axis, dim):
    peers = lax.axis_size(axis)
    tiles = lax.all_to_all(split_up(array, dim, peers), axis, 0, 0, tiled=True)
    return jnp.sum(tiles, axis=0)


def apply_tiles(u_rows, v_rows, expanded):
    n_items = v_rows.shape[0]
    rank_most = v_rows.shape[1]
    flat_v = v_rows.reshape(n_items, rank_most, -1)
    projected = lax.dot_general(
        flat_v, expanded, (((2,), (1,)), ((0,), (0,))), preferred_element_type=jnp.float32
    )
    projected = projected.astype(jnp.bfloat16)
    half_cols = projected.shape[2] // 2
    w_real = projected[:, :, :half_cols]
    w_imag = projected[:, :, half_cols:]
    stacked = jnp.concatenate([projected, jnp.concatenate([-w_imag, w_real], axis=2)], axis=1)
    flat_u = u_rows.reshape(n_items, 2 * rank_most, -1)
    result = lax.dot_general(
        flat_u, stacked, (((1,), (1,)), ((0,), (0,))), preferred_element_type=jnp.float32
    )
    return result.astype(jnp.bfloat16)


def widen_blocks(real_part, imag_part):
    upper = jnp.concatenate([real_part, imag_part], axis=2)
    lower = jnp.concatenate([imag_part, -real_part], axis=2)
    return jnp.concatenate([upper, lower], axis=1)


def body(field, u_basis, v_basis, tile_ranks, window_start):
    n_src = lax.axis_size("src")
    levels = u_basis.shape[2]
    col_tiles = u_basis.shape[3]
    rank_most = u_basis.shape[5]
    tile_size = u_basis.shape[6]
    columns = field.shape[2]
    spacing = n_src // col_tiles
    capacity = AR // spacing
    holder = lax.axis_index("src")
    local_u = u_basis.reshape(levels * col_tiles, 2, rank_most, tile_size)
    local_v = v_basis.reshape(levels * col_tiles, rank_most, 2, tile_size)
    rank_list = tile_ranks.reshape(levels * col_tiles)
    rank_keep = jnp.arange(rank_most, dtype=jnp.int32)[None, :] < rank_list[:, None]
    masked_v = jnp.where(rank_keep[:, :, None, None], local_v, jnp.zeros_like(local_v))
    col_ids = jnp.arange(col_tiles, dtype=jnp.int32)
    offsets = (holder - spacing * col_ids[None, :] - window_start[:, None]) % n_src
    inside = offsets < AR
    row_ids = window_start[:, None] + offsets
    tile_ids = row_ids // n_src * col_tiles + col_ids[None, :]
    slot_pos = jnp.cumsum(inside.astype(jnp.int32), axis=1) - 1
    slot_range = jnp.arange(capacity, dtype=jnp.int32)
    slot_match = inside[:, None, :] & (slot_pos[:, None, :] == slot_range[None, :, None])
    picked = jnp.sum(jnp.where(slot_match, tile_ids[:, None, :], 0), axis=2).reshape(-1)
    window_first = window_start[holder]
    t_ids = jnp.arange(AR, dtype=jnp.int32)
    sources = (window_first + t_ids[None, :] + spacing * col_ids[:, None]) % n_src
    earlier = (sources[:, :, None] - spacing * col_ids[None, None, :] - window_first) % n_src < AR
    before = col_ids[None, None, :] < col_ids[:, None, None]
    entries = jnp.sum((earlier & before).astype(jnp.int32), axis=2)
    item_ids = sources * capacity + entries
    blocks = field.reshape(2, col_tiles, tile_size, columns)
    slot_ids = jnp.arange(n_src * capacity, dtype=jnp.int32)
    slot_hit = item_ids[None, :, :] == slot_ids[:, None, None]
    slot_col = jnp.sum(jnp.where(slot_hit, col_ids[None, :, None], 0), axis=(1, 2))
    raw_blocks = jnp.swapaxes(blocks, 0, 1)
    send_f = jnp.take(raw_blocks, slot_col, axis=0)
    got_f = lax.all_to_all(send_f, "src", split_axis=0, concat_axis=0, tiled=True)
    widened = widen_blocks(got_f[:, 0], got_f[:, 1])
    own_u = jnp.take(local_u, picked, axis=0)
    own_v = jnp.take(masked_v, picked, axis=0)
    tile_out = apply_tiles(own_u, own_v, widened)
    returned = lax.all_to_all(tile_out, "src", split_axis=0, concat_axis=0, tiled=True)
    ordering = jnp.transpose(item_ids).reshape(-1)
    gathered = jnp.take(returned, ordering, axis=0).reshape(AR, col_tiles, tile_size, 2 * columns)
    accum = jnp.sum(gathered.astype(jnp.float32), axis=1)
    flat_rows = accum.reshape(AR * tile_size, 2 * columns)
    own_rows = sent_and_summed(flat_rows, "rcv", 0)
    rounded = own_rows.astype(jnp.bfloat16)
    return rounded.reshape(-1, 2, columns).transpose(1, 0, 2)


def solution(mesh):
    return jax.shard_map(
        body,
        mesh=mesh,
        in_specs=(
            P(None, "rcv", "src"),
            P("src", "rcv", None, None, None, None, None),
            P("src", "rcv", None, None, None, None, None),
            P("src", "rcv", None, None),
            P(),
        ),
        out_specs=P(None, "rcv", "src"),
        check_vma=False,
    )
```

profile of v0, /device:TPU:1, one launch (start us, length us, event | category | flops | bytes accessed | tf_op | source)
XLA Modules:
  0.0 513.7 jit_solution(5650432245634064259)
XLA Ops:
  0.0 1.4 dynamic_slice.3
  1.4 0.6 iota_multiply_fusion
  2.1 0.9 convert_reduce_fusion.1
  3.2 0.1 select_reduce_fusion
  3.3 2.3 copy.30
  5.6 6.9 %gather_fusion.2 = bf16[64,2,256,128]{3,2,1,0:T(8,128)(2,1)} fusion(bf16[8,2,256,128]{3,2,1,0:T(8,128)(2,1)} %bitcast.38, s32[1024]{0:T(1024)S(1)} %pad_clamp_fusion.1), kind=kCustom, calls=%fused_computation.2 | custom fusion | bytes 16777472 | tf_op jit(solution)/shard_map/jit(_take)/gather | solution.py:81
  12.5 7.6 %broadcast_select_fusion = bf16[64,2,256,128]{3,2,1,0:T(8,128)(2,1)} fusion(bf16[64,2,256,128]{3,2,1,0:T(8,128)(2,1)} %gather_fusion.2, pred[64]{0:T(512)(128)(4,1)S(1)} %compare_and_fusion.1), kind=kLoop, calls=%fused_computation.22 | loop fusion | flops 4194304 | bytes 16777280 | tf_op jit(solution)/shard_map/jit(_take)/select_n | solution.py:81
  20.1 12.5 %all-to-all-start = ((bf16[64,2,256,128]{3,2,1,0:T(8,128)(2,1)}), bf16[64,2,256,128]{3,2,1,0:T(8,128)(2,1)}, u32[]{:S(2)}, u32[]{:S(2)}) async-start(bf16[64,2,256,128]{3,2,1,0:T(8,128)(2,1)} %broadcast_select_fusion), calls=%async_computation | async-start | bytes 16777216 | tf_op jit(solution)/shard_map/all_to_all | solution.py:82
  32.7 0.1 fusion.33
  32.8 0.1 copy.20
  32.9 0.1 reshape.380
  33.0 0.1 reshape.378
  33.3 7.3 %broadcast_select_fusion.1 = bf16[16,160,2,256]{3,2,1,0:T(2,128)(2,1)} fusion(pred[16,160]{1,0:T(8,128)(4,1)S(1)} %iota_compare_fusion.1, bf16[1,1,2,8,160,2,256]{6,5,4,3,2,1,0:T(2,128)(2,1)} %param.7), kind=kLoop, calls=%fused_computation.25 | loop fusion | flops 1310720 | bytes 5245440 | tf_op jit(solution)/shard_map/jit(_where)/select_n | solution.py:59
  40.6 24.6 %gather_fusion.1 = bf16[64,160,2,256]{3,2,1,0:T(2,128)(2,1)} fusion(bf16[16,160,2,256]{3,2,1,0:T(2,128)(2,1)} %broadcast_select_fusion.1, s32[1024]{0:T(1024)S(1)} %pad_clamp_fusion.2), kind=kCustom, calls=%fused_computation.1 | custom fusion | bytes 20971776 | tf_op jit(solution)/shard_map/jit(_take)/gather | solution.py:85
  65.2 17.3 %gather.25 = bf16[64,160,512]{2,1,0:T(8,128)(2,1)} reshape(bf16[64,160,2,256]{3,2,1,0:T(2,128)(2,1)} %gather_fusion.1) | data formatting | bytes 20971520 | tf_op jit(solution)/shard_map/jit(_take)/gather | solution.py:85
  82.6 6.5 %gather_fusion = bf16[64,2,160,256]{3,2,1,0:T(8,128)(2,1)} fusion(bf16[16,2,160,256]{3,2,1,0:T(8,128)(2,1)S(1)} %bitcast.37, s32[1024]{0:T(1024)S(1)} %pad_clamp_fusion.2), kind=kCustom, calls=%fused_computation | custom fusion | bytes 20971776 | tf_op jit(solution)/shard_map/jit(_take)/gather | solution.py:84
  89.1 10.1 %bitcast_select_fusion = bf16[64,320,256]{2,1,0:T(8,128)(2,1)} fusion(bf16[64,2,160,256]{3,2,1,0:T(8,128)(2,1)} %gather_fusion, pred[64]{0:T(512)(128)(4,1)S(1)} %compare_and_fusion.2), kind=kLoop, calls=%fused_computation.19 | loop fusion | flops 5242880 | bytes 20971584 | tf_op jit(solution)/shard_map/jit(_take)/select_n | solution.py:84
  99.2 117.7 %all-to-all-done = bf16[64,2,256,128]{3,2,1,0:T(8,128)(2,1)} async-done(((bf16[64,2,256,128]{3,2,1,0:T(8,128)(2,1)}), bf16[64,2,256,128]{3,2,1,0:T(8,128)(2,1)}, u32[]{:S(2)}, u32[]{:S(2)}) %all-to-all-start) | async-done | bytes 8388640 | tf_op jit(solution)/shard_map/all_to_all | solution.py:82
  216.9 4.8 fusion.46
  221.7 6.0 %slice_bitcast_fusion.1 = (bf16[64,256,128]{2,1,0:T(8,128)(2,1)}, bf16[64,256,128]{2,1,0:T(8,128)(2,1)}) fusion(bf16[64,2,256,128]{3,2,1,0:T(8,128)(2,1)} %all-to-all-done), kind=kLoop, calls=%fused_computation.27 | loop fusion | bytes 16777216 | tf_op jit(solution)/shard_map/squeeze | solution.py:83
  227.7 12.8 %fusion.20 = bf16[64,160,256]{2,1,0:T(8,128)(2,1)} fusion(bf16[64,256,128]{2,1,0:T(8,128)(2,1)} %fusion.46, bf16[64,256,128]{2,1,0:T(8,128)(2,1)} %get-tuple-element.8, bf16[64,256,128]{2,1,0:T(8,128)(2,1)} %get-tuple-element.7, bf16[64,160,512]{2,1,0:T(8,128)(2,1)} %gather.25, pred[64]{0:T(512)(128)(4,1)S(1)} %compare_and_fusion.2), kind=kOutput, calls=%fused_computation.28 | convolution fusion | flops 2759327744 | bytes 28311616 | tf_op jit(solution)/shard_map/dot_general | solution.py:24
  240.4 4.5 slice_negate_fusion
  244.9 10.8 %fusion.16 = bf16[64,256,256]{2,1,0:T(8,128)(2,1)} fusion(bf16[64,320,256]{2,1,0:T(8,128)(2,1)} %bitcast_select_fusion, bf16[64,160,128]{2,1,0:T(8,128)(2,1)} %get-tuple-element.10, bf16[64,160,128]{2,1,0:T(8,128)(2,1)S(1)} %get-tuple-element.9, bf16[64,160,256]{2,1,0:T(8,128)(2,1)} %fusion.20), kind=kOutput, calls=%fused_computation.23 | convolution fusion | flops 2720006144 | bytes 29360128 | tf_op jit(solution)/shard_map/dot_general | solution.py:33
  255.7 18.8 %all-to-all-start.1 = ((bf16[64,256,256]{2,1,0:T(8,128)(2,1)}), bf16[64,256,256]{2,1,0:T(8,128)(2,1)}, u32[]{:S(2)}, u32[]{:S(2)}) async-start(bf16[64,256,256]{2,1,0:T(8,128)(2,1)} %fusion.16), calls=%async_computation.1 | async-start | bytes 16777216 | tf_op jit(solution)/shard_map/all_to_all | solution.py:87
  274.6 0.1 compare_and_fusion
  274.8 186.3 %all-to-all-done.1 = bf16[64,256,256]{2,1,0:T(8,128)(2,1)} async-done(((bf16[64,256,256]{2,1,0:T(8,128)(2,1)}), bf16[64,256,256]{2,1,0:T(8,128)(2,1)}, u32[]{:S(2)}, u32[]{:S(2)}) %all-to-all-start.1) | async-done | bytes 8388640 | tf_op jit(solution)/shard_map/all_to_all | solution.py:87
  461.1 8.9 %gather_fusion.3 = bf16[64,256,256]{2,1,0:T(8,128)(2,1)} fusion(bf16[64,256,256]{2,1,0:T(8,128)(2,1)} %all-to-all-done.1, s32[1024]{0:T(1024)S(1)} %pad_clamp_fusion), kind=kCustom, calls=%fused_computation.3 | custom fusion | bytes 16777472 | tf_op jit(solution)/shard_map/jit(_take)/gather | solution.py:89
  470.0 6.4 %convert_reduce_fusion = f32[8,256,256]{2,1,0:T(8,128)S(1)} fusion(pred[8,8]{1,0:T(8,128)(4,1)S(1)} %get-tuple-element.5, bf16[64,256,256]{2,1,0:T(8,128)(2,1)} %gather_fusion.3), kind=kLoop, calls=%fused_computation.12 | loop fusion | flops 12058624 | bytes 10485824 | tf_op jit(solution)/shard_map/reduce_sum | solution.py:90
  476.4 34.7 %all_to_all.15 = f32[8,256,256]{2,1,0:T(8,128)} all-to-all(f32[8,256,256]{2,1,0:T(8,128)S(1)} %convert_reduce_fusion), channel_id=1, replica_groups=mesh['src'=32,'rcv'=8] {'rcv'}, dimensions={0} | all-to-all | bytes 4194304 | tf_op jit(solution)/shard_map/all_to_all | solution.py:16
  511.1 1.7 reduce_sum.55
  512.8 0.1 copy.25
  512.9 0.8 copy.26
  (27 shorter events, 0.7 us)
Async XLA Ops:
  0.0 82.6 %copy-start = (bf16[1,1,2,8,2,160,256]{6,5,4,3,2,1,0:T(8,128)(2,1)S(1)}, bf16[1,1,2,8,2,160,256]{6,5,4,3,2,1,0:T(8,128)(2,1)}, u32[]{:S(2)}) copy-start(bf16[1,1,2,8,2,160,256]{6,5,4,3,2,1,0:T(8,128)(2,1)} %param.6) | copy-start | bytes 7864324
  20.1 12.5 %copy-start.2 = (s32[32]{0:T(128)S(1)}, s32[32]{0:T(128)}, u32[]{:S(2)}) copy-start(s32[32]{0:T(128)} %param.9) | copy-start | bytes 388
  20.1 13.0 %copy-start.3 = (s32[1,1,2,8]{3,2,1,0:T(2,128)S(1)}, s32[1,1,2,8]{3,2,1,0:T(2,128)}, u32[]{:S(2)}) copy-start(s32[1,1,2,8]{3,2,1,0:T(2,128)} %param.8) | copy-start | bytes 196
  20.1 196.8 %all-to-all-start = ((bf16[64,2,256,128]{3,2,1,0:T(8,128)(2,1)}), bf16[64,2,256,128]{3,2,1,0:T(8,128)(2,1)}, u32[]{:S(2)}, u32[]{:S(2)}) async-start(bf16[64,2,256,128]{3,2,1,0:T(8,128)(2,1)} %broadcast_select_fusion), calls=%async_computation | async-start | bytes 16777216 | tf_op jit(solution)/shard_map/all_to_all | solution.py:82
  255.7 205.3 %all-to-all-start.1 = ((bf16[64,256,256]{2,1,0:T(8,128)(2,1)}), bf16[64,256,256]{2,1,0:T(8,128)(2,1)}, u32[]{:S(2)}, u32[]{:S(2)}) async-start(bf16[64,256,256]{2,1,0:T(8,128)(2,1)} %fusion.16), calls=%async_computation.1 | async-start | bytes 16777216 | tf_op jit(solution)/shard_map/all_to_all | solution.py:87
  470.0 43.7 %copy-start.1 = (bf16[1,1,2,8,2,160,256]{6,5,4,3,2,1,0:T(8,128)(2,1)S(1)}, bf16[1,1,2,8,2,160,256]{6,5,4,3,2,1,0:T(8,128)(2,1)}, u32[]{:S(2)}) copy-start(bf16[1,1,2,8,2,160,256]{6,5,4,3,2,1,0:T(8,128)(2,1)} %param.6) | copy-start | bytes 7864324
where the time goes:
time: 515 us; the launch traced here: 514 us
  waiting for transfers between devices  304 us (59%)
  local copies, waits for them, and re-layouts  75.3 us (15%)
  other arithmetic  44.8 us (9%)
  blocking collectives  34.7 us (7%)
  starting transfers between devices  31.3 us (6%)
  matrix products  23.6 us (5%)
    all_to_all x1, waiting for transfers between devices, body(): lax.all_to_all(tile_out, 'src', split_axis=0, concat_axis=0, tiled=True)  186 us
    all_to_all x1, waiting for transfers between devices, body(): lax.all_to_all(send_f, 'src', split_axis=0, concat_axis=0, tiled=True)  118 us
    gather x2, local copies, waits for them, and re-layouts, body(): own_v = jnp.take(masked_v, picked, axis=0)  41.9 us
    all_to_all x1, blocking collectives, sent_and_summed(): tiles = lax.all_to_all(split_up(array, dim, peers), axis, 0, 0, tiled=True)  34.7 us
    all_to_all x1, starting transfers between devices, body(): lax.all_to_all(tile_out, 'src', split_axis=0, concat_axis=0, tiled=True)  18.8 us
    dot_general x1, matrix products, apply_tiles(): lax.dot_general(flat_v, expanded, (((2,), (1,)), ((0,), (0,))), preferred...  12.8 us
    all_to_all x1, starting transfers between devices, body(): lax.all_to_all(send_f, 'src', split_axis=0, concat_axis=0, tiled=True)  12.5 us
    dot_general x1, matrix products, apply_tiles(): lax.dot_general(flat_u, stacked, (((1,), (1,)), ((0,), (0,))), preferred_...  10.8 us
  transfers between devices with their start and end apart: 2, of which 2 were waited for; matrix products, arithmetic and copies ran while one was open for 13% of the time, Pallas kernels for 0%

commit v1 on v0

v1 whole, which is shorter than its diff:
```python
import jax
import jax.numpy as jnp
from jax import lax
from jax.experimental import pallas as pl
from jax.experimental.pallas import tpu as pltpu
from jax.sharding import PartitionSpec as P

MESH = pl.DeviceIdType.MESH
BF = jnp.bfloat16
F32 = jnp.float32
NZ, NY, NX = 8, 4, 4
STEPS = 8


def rem(a, b):
    return lax.rem(a, jnp.int32(b))


def div(a, b):
    return lax.div(a, jnp.int32(b))


def kernel(
    field_ref, u_ref, v_ref, rank_ref, ws_ref, out_ref,
    fbuf, gx, zb, mids, oths, osend, relay, terms, crecv, xs, xr, zsb, zr, fin, fr,
    uraw, vraw, ut, v2,
    lsem, zss, zrs, yss, yrs, css, crs, xss, xrs, gss, grs, fss, frs,
):
    src = lax.axis_index("src")
    rcv = lax.axis_index("rcv")
    z, y = div(src, NY), rem(src, NY)
    x, core = div(rcv, 2), rem(rcv, 2)

    def zdev(offset):
        return (rem(z + (offset + 2 * NZ), NZ) * NY + y, rcv)

    def ydev(offset):
        return (z * NY + rem(y + (offset + NY), NY), rcv)

    sibling = (src, x * 2 + 1 - core)

    def rcopy(source, target, ss, rs, device):
        return pltpu.make_async_remote_copy(
            src_ref=source, dst_ref=target, send_sem=ss, recv_sem=rs,
            device_id=device, device_id_type=MESH,
        )

    load_f = pltpu.make_async_copy(field_ref, fbuf, lsem.at[0])
    load_v = pltpu.make_async_copy(v_ref, vraw, lsem.at[1])
    load_u = pltpu.make_async_copy(u_ref, uraw, lsem.at[2])
    load_f.start()
    load_v.start()
    load_u.start()

    barrier = pltpu.get_barrier_semaphore()
    for offset in range(1, NZ):
        pl.semaphore_signal(barrier, inc=1, device_id=zdev(offset), device_id_type=MESH)
    for offset in range(1, NY):
        pl.semaphore_signal(barrier, inc=1, device_id=ydev(offset), device_id_type=MESH)
    pl.semaphore_signal(barrier, inc=1, device_id=sibling, device_id_type=MESH)
    for offset in range(1, NX):
        pl.semaphore_signal(
            barrier, inc=1, device_id=(src, rem(x + offset, NX) * 2 + core), device_id_type=MESH
        )
    for k in range(4):
        t_src, t_rcv = z * NY + x, core * 4 + k

        @pl.when(jnp.logical_or(t_src != src, t_rcv != rcv))
        def _():
            pl.semaphore_signal(barrier, inc=1, device_id=(t_src, t_rcv), device_id_type=MESH)

        s_src, s_rcv = z * NY + k, y * 2 + div(x, 2)

        @pl.when(jnp.logical_or(s_src != src, s_rcv != rcv))
        def _():
            pl.semaphore_signal(barrier, inc=1, device_id=(s_src, s_rcv), device_id_type=MESH)

    own_final = jnp.where(jnp.logical_and(x == y, div(x, 2) == core), 1, 0).astype(jnp.int32)

    load_f.wait()
    shift = z + 19 - lax.shift_right_logical(ws_ref[src], jnp.int32(2))

    def roll_block(j, carry):
        block = lax.bitwise_and(shift + j, jnp.int32(7))
        gx[j, :, 0:128] = fbuf[0, block]
        gx[j, :, 128:256] = fbuf[1, block]
        return carry

    lax.fori_loop(0, 10, roll_block, 0)
    pl.semaphore_wait(barrier, 14 + 8 - 2 * own_final)

    def plane(m):
        h = div(m + 1, 2)
        odd = rem(m, 2)
        return rem(z + 8 + h - 2 * h * odd, NZ)

    def zcopy(source, m, kk, direction):
        return rcopy(source, zb.at[m - 1, kk], zss.at[m - 1, kk], zrs.at[m - 1, kk], zdev(direction))

    def ycopy(m, i, mid=None):
        toward = ydev(-1) if i in (3, 4, 5, 8, 9) else ydev(1)
        top, low = pl.ds(0, 128), pl.ds(128, 128)
        if i in (0, 3):
            source, target = (mids.at[m, 0] if mid is None else mid), mids.at[m, 3 if i == 0 else 1]
        elif i == 1:
            source, target = osend.at[m, 0], oths.at[m, 3]
        elif i == 2:
            source, target = osend.at[m, 2, top], relay.at[m, 0]
        elif i == 4:
            source, target = osend.at[m, 1], oths.at[m, 1]
        elif i == 5:
            source, target = osend.at[m, 2, low], relay.at[m, 1]
        elif i == 6:
            source, target = mids.at[m, 3, top], mids.at[m, 2, top]
        elif i == 7:
            source, target = relay.at[m, 0], oths.at[m, 2, top]
        elif i == 8:
            source, target = mids.at[m, 1, low], mids.at[m, 2, low]
        else:
            source, target = relay.at[m, 1], oths.at[m, 2, low]
        return rcopy(source, target, yss.at[m, i], yrs.at[m, i], toward)

    def ysend(m, mid, upper, lower):
        reader = plane(m) * NY + y
        phase = lax.bitwise_and(ws_ref[reader], jnp.int32(3))

        def rows(i, carry):
            at = pl.ds(pl.multiple_of(i * 32, 32), 32)
            mids[m, 0, at] = mid[at]
            one, two = upper[at], lower[at]
            for k, target in enumerate((oths.at[m, 0], osend.at[m, 0], osend.at[m, 1], osend.at[m, 2])):
                side = rem(y + (0, 1, 3, 2)[k], NY)
                target[at] = jnp.where(side >= phase, one, two)
            return carry

        lax.fori_loop(0, 8, rows, 0)
        for i in (0, 3, 2, 5, 1, 4):
            ycopy(m, i, mid).start()

    def yrelay(m):
        for came, onward in ((0, 6), (3, 8), (2, 7), (5, 9)):
            ycopy(m, came).wait_recv()
            ycopy(m, onward).start()

    def zneeded(m):
        h = div(m + 1, 2)

        @pl.when(rem(m, 2) == 1)
        def _():
            for i in range(3):
                kk = h - 1 + i
                zcopy(zb.at[m - 1, kk], m, kk, 1).wait_recv()
                if i > 0:
                    @pl.when(h < 4)
                    def _():
                        zcopy(zb.at[m - 1, kk], m + 2, kk, 1).start()
            ysend(m, zb.at[m - 1, h], zb.at[m - 1, h + 1], zb.at[m - 1, h - 1])

        @pl.when(rem(m, 2) == 0)
        def _():
            for i in range(3):
                kk = 5 - h - i
                zcopy(zb.at[m - 1, kk], m, kk, -1).wait_recv()
                if i > 0:
                    @pl.when(h < 3)
                    def _():
                        zcopy(zb.at[m - 1, kk], m + 2, kk, -1).start()
            ysend(m, zb.at[m - 1, 4 - h], zb.at[m - 1, 5 - h], zb.at[m - 1, 3 - h])

    def zrest(m):
        h = div(m + 1, 2)

        @pl.when(rem(m, 2) == 1)
        def _():
            def go(kk, carry):
                zcopy(zb.at[m - 1, kk], m, kk, 1).wait_recv()
                zcopy(zb.at[m - 1, kk], m + 2, kk, 1).start()
                return carry

            lax.fori_loop(h + 2, 6, go, 0)

        @pl.when(rem(m, 2) == 0)
        def _():
            def go(i, carry):
                kk = 2 - h - i
                zcopy(zb.at[m - 1, kk], m, kk, -1).wait_recv()
                zcopy(zb.at[m - 1, kk], m + 2, kk, -1).start()
                return carry

            lax.fori_loop(0, 3 - h, go, 0)

    def ccopy(m, k):
        return rcopy(terms.at[0, m, k], crecv.at[m, k], css.at[m, k], crs.at[m, k], sibling)

    def compute(m):
        first = plane(m) * NY

        def unit(i, carry):
            k = i + jnp.where(i == 2, 1, 0) - jnp.where(i == 3, 1, 0)
            @pl.when(k == 1)
            def _():
                ycopy(m, 4).wait_recv()

            @pl.when(k == 3)
            def _():
                ycopy(m, 1).wait_recv()

            @pl.when(k == 2)
            def _():
                for j in range(6, 10):
                    ycopy(m, j).wait_recv()

            start = ws_ref[first + rem(y + k, NY)]
            phase = lax.bitwise_and(start, jnp.int32(3))
            late = jnp.where(y < phase, 1, 0).astype(jnp.int32)
            group = lax.shift_right_logical(start, jnp.int32(2)) + late
            column = lax.bitwise_and(z + 16 - group, jnp.int32(7))
            row = group * 4 + y
            tile0 = lax.shift_right_logical(row, jnp.int32(5)) * 8 + column
            tile1 = lax.shift_right_logical(row + 4, jnp.int32(5)) * 8 + lax.bitwise_and(column + 7, jnp.int32(7))

            def item(w, inner):
                e = rem(core + 1 + w, 2)
                tile = jnp.where(e == 0, tile0, tile1)
                block = jnp.where(e + late == 1, mids[m, k], oths[m, k])
                parts = jnp.dot(v2[tile], block, preferred_element_type=F32)
                w_real = (parts[:160, :128] + parts[160:, 128:]).astype(BF)
                w_imag = (parts[:160, 128:] - parts[160:, :128]).astype(BF)
                stacked = jnp.concatenate(
                    [
                        jnp.concatenate([w_real, w_imag], axis=1),
                        jnp.concatenate([-w_imag, w_real], axis=1),
                    ],
                    axis=0,
                )
                terms[w, m, k] = jnp.dot(ut[tile], stacked, preferred_element_type=F32).astype(BF)
                return inner

            lax.fori_loop(0, 2, item, 0)
            ccopy(m, k).start()
            return carry

        lax.fori_loop(0, 4, unit, 0)

    def xcopy(m, k):
        owner = rem(y + k, NY)
        slot = rem(x + NX - owner, NX) - 1
        return rcopy(xs.at[m, k], xr.at[m, slot], xss.at[m, k], xrs.at[m, slot], (src, owner * 2 + core))

    def core_sum(m):
        def unit(k, carry):
            ccopy(m, k).wait_recv()
            xs[m, k] = (terms[1, m, k].astype(F32) + crecv[m, k].astype(F32)).astype(BF)
            return carry

        lax.fori_loop(0, 4, unit, 0)

        def send(k, carry):
            @pl.when(rem(y + k, NY) != x)
            def _():
                xcopy(m, k).start()

            return carry

        lax.fori_loop(0, 4, send, 0)

    def gcopy(m):
        return rcopy(zsb.at[m], zr.at[m], gss.at[m], grs.at[m], (plane(m) * NY + y, rcv))

    def x_sum(m):
        for j in range(3):
            rcopy(xr.at[m, j], xr.at[m, j], xss.at[m, 0], xrs.at[m, j], sibling).wait_recv()
        total = xs[m, rem(x + NY - y, NY)].astype(F32)
        for j in range(3):
            total = total + xr[m, j].astype(F32)
        zsb[m] = total.astype(BF)

        @pl.when(m > 0)
        def _():
            gcopy(m).start()

    for i in range(6):
        zcopy(gx.at[i + 4], 1, i, 1).start()
        if i < 5:
            zcopy(gx.at[4 - i], 2, 4 - i, -1).start()
    ysend(jnp.int32(0), gx.at[4], gx.at[5], gx.at[3])

    load_v.wait()
    load_u.wait()

    def prepare(t, carry):
        keep = lax.broadcasted_iota(jnp.int32, (160, 256), 0) < rank_ref[t]
        for c in range(2):
            part = vraw[t, :, c, :]
            v2[t, c * 160:(c + 1) * 160, :] = jnp.where(keep, part, jnp.zeros_like(part))
        ut[t] = jnp.transpose(uraw[t])
        return carry

    lax.fori_loop(0, 16, prepare, 0)
    yrelay(jnp.int32(0))
    zneeded(jnp.int32(1))

    def step(n, carry):
        @pl.when(n < 7)
        def _():
            yrelay(n + 1)

        @pl.when(n < 6)
        def _():
            zneeded(n + 2)

        @pl.when(n < 8)
        def _():
            compute(n)

        @pl.when(n == 0)
        def _():
            zrest(n + 1)

        @pl.when(n < 5)
        def _():
            zrest(n + 2)

        @pl.when(jnp.logical_and(n > 0, n < 9))
        def _():
            core_sum(n - 1)

        @pl.when(n > 1)
        def _():
            x_sum(n - 2)

        return carry

    lax.fori_loop(0, STEPS + 2, step, 0)

    total = zsb[0].astype(F32)
    for m in range(1, STEPS):
        gcopy(jnp.int32(m)).wait_recv()
        total = total + zr[m].astype(F32)
    fin[...] = total.astype(BF)

    def fcopy(k):
        return rcopy(fin, fr.at[y], fss.at[k], frs.at[y], (z * NY + x, core * 4 + k))

    def mine(k):
        return jnp.logical_and(x == y, core * 4 + k == rcv)

    for k in range(4):
        @pl.when(jnp.logical_not(mine(k)))
        def _():
            fcopy(k).start()

        @pl.when(mine(k))
        def _():
            fr[y] = fin[...]

    for k in range(4):
        @pl.when(jnp.logical_or(y != k, own_final == 0))
        def _():
            rcopy(fin, fr.at[k], fss.at[k], frs.at[k], sibling).wait_recv()

    turn = lax.bitwise_and(rem(rcv, 4) + ws_ref[src], jnp.int32(3))
    result = fr[turn]
    out_ref[0] = result[:, 0:128]
    out_ref[1] = result[:, 128:256]

    for k in range(4):
        @pl.when(jnp.logical_not(mine(k)))
        def _():
            fcopy(k).wait_send()

    for i in range(6):
        zcopy(gx.at[i + 4], 1, i, 1).wait_send()
        if i < 5:
            zcopy(gx.at[4 - i], 2, 4 - i, -1).wait_send()

    def drain(m, carry):
        for i in range(10):
            ycopy(m, i).wait_send()

        def inner(k, c):
            ccopy(m, k).wait_send()

            @pl.when(rem(y + k, NY) != x)
            def _():
                xcopy(m, k).wait_send()

            return c

        lax.fori_loop(0, 4, inner, 0)

        @pl.when(m > 0)
        def _():
            gcopy(m).wait_send()

        h = div(m + 1, 2)

        @pl.when(jnp.logical_and(rem(m, 2) == 1, h > 1))
        def _():
            def go(kk, c):
                zcopy(zb.at[0, kk], m, kk, 1).wait_send()
                return c

            lax.fori_loop(h - 1, 6, go, 0)

        @pl.when(jnp.logical_and(rem(m, 2) == 0, h > 1))
        def _():
            def go(kk, c):
                zcopy(zb.at[0, kk], m, kk, -1).wait_send()
                return c

            lax.fori_loop(0, 6 - h, go, 0)

        return carry

    lax.fori_loop(0, STEPS, drain, 0)


def body(field, u_basis, v_basis, tile_ranks, window_start):
    fields = field.reshape(2, 8, 256, 128)
    u_tiles = u_basis.reshape(16, 320, 256)
    v_tiles = v_basis.reshape(16, 160, 2, 256)
    ranks = tile_ranks.reshape(16)

    def blocks(*lead):
        return pltpu.VMEM((*lead, 256, 256), BF)

    def sems(*shape):
        return pltpu.SemaphoreType.DMA(shape)

    anywhere = pl.BlockSpec(memory_space=pl.ANY)
    scalars = pl.BlockSpec(memory_space=pltpu.SMEM)
    return pl.pallas_call(
        kernel,
        out_shape=jax.ShapeDtypeStruct((2, 256, 128), BF),
        in_specs=[anywhere, anywhere, anywhere, scalars, scalars],
        out_specs=pl.BlockSpec(memory_space=pltpu.VMEM),
        scratch_shapes=[
            pltpu.VMEM((2, 8, 256, 128), BF),
            blocks(10), blocks(7, 6), blocks(8, 4), blocks(8, 4), blocks(8, 3),
            pltpu.VMEM((8, 2, 128, 256), BF),
            blocks(2, 8, 4), blocks(8, 4), blocks(8, 4), blocks(8, 3), blocks(8), blocks(8),
            blocks(), blocks(4),
            pltpu.VMEM((16, 320, 256), BF),
            pltpu.VMEM((16, 160, 2, 256), BF),
            pltpu.VMEM((16, 256, 320), BF),
            pltpu.VMEM((16, 320, 256), BF),
            sems(3), sems(7, 6), sems(7, 6), sems(8, 10), sems(8, 10), sems(8, 4), sems(8, 4),
            sems(8, 4), sems(8, 3), sems(8), sems(8), sems(4), sems(4),
        ],
        compiler_params=pltpu.CompilerParams(
            collective_id=0, has_side_effects=True, vmem_limit_bytes=60 * 1024 * 1024
        ),
    )(fields, u_tiles, v_tiles, ranks, window_start)


def solution(mesh):
    return jax.shard_map(
        body,
        mesh=mesh,
        in_specs=(
            P(None, "rcv", "src"),
            P("src", "rcv", None, None, None, None, None),
            P("src", "rcv", None, None, None, None, None),
            P("src", "rcv", None, None),
            P(),
        ),
        out_specs=P(None, "rcv", "src"),
        check_vma=False,
    )
```

time: 515 us -> 142 us (0.28)
  waiting for transfers between devices: 304 us -> 0 us
  Pallas kernels: 0 us -> 137 us
  local copies, waits for them, and re-layouts: 75.3 us -> 2.84 us
  other arithmetic: 44.8 us -> 0 us
  blocking collectives: 34.7 us -> 0 us
  starting transfers between devices: 31.3 us -> 0 us
  matrix products: 23.6 us -> 0 us
    all_to_all x2 -> x0, waiting for transfers between devices: 304 us -> none  [the longest x1 186 us: body(): lax.all_to_all(tile_out, 'src', split_axis=0, concat_axis=0, tiled=True)]
    pallas_call x0 -> x1, Pallas kernels: none -> 137 us  [body(): pl.pallas_call(kernel, out_shape=jax.ShapeDtypeStruct((2, 256, 128), BF),...]
    gather x5 -> x0, local copies, waits for them, and re-layouts: 64.2 us -> none  [the longest x2 41.9 us: body(): own_v = jnp.take(masked_v, picked, axis=0)]
    all_to_all x1 -> x0, blocking collectives: 34.7 us -> none  [sent_and_summed(): tiles = lax.all_to_all(split_up(array, dim, peers), axis, 0, 0, tiled=True)]
    all_to_all x2 -> x0, starting transfers between devices: 31.3 us -> none  [the longest x1 18.8 us: body(): lax.all_to_all(tile_out, 'src', split_axis=0, concat_axis=0, tiled=True)]
    select_n x7 -> x0, other arithmetic: 25.1 us -> none  [the longest x2 10.1 us: body(): own_u = jnp.take(local_u, picked, axis=0)]
    dot_general x2 -> x0, matrix products: 23.6 us -> none  [the longest x1 12.8 us: apply_tiles(): lax.dot_general(flat_v, expanded, (((2,), (1,)), ((0,), (0,))), preferred...]
    neg x2 -> x0, other arithmetic: 9.32 us -> none  [the longest x1 4.81 us: widen_blocks(): lower = jnp.concatenate([imag_part, -real_part], axis=2)]
  transfers between devices with their start and end apart: 2 -> 0, of which waited for: 2 -> 0; matrix products, arithmetic and copies ran while one was open for 13% -> 0% of each run, Pallas kernels for 0% -> 0%
where the time goes in v1:
time: 142 us; the launch traced here: 140 us
  Pallas kernels  137 us (96%)
  local copies, waits for them, and re-layouts  2.84 us (2%)
    pallas_call x1, Pallas kernels, body(): pl.pallas_call(kernel, out_shape=jax.ShapeDtypeStruct((2, 256, 128), BF),...  137 us

profile of v1, /device:TPU:1, one launch (start us, length us, event | category | flops | bytes accessed | tf_op | source)
XLA Modules:
  0.0 140.2 jit_solution(12428492653423875127)
XLA Ops:
  0.0 1.3 reshape.15.rank_ref
  1.3 137.4 %shard_map.55 = bf16[2,256,128]{2,1,0:T(8,128)(2,1)} custom-call(bf16[2,8,256,128]{3,2,1,0:T(8,128)(2,1)} %bitcast.5, bf16[16,320,256]{2,1,0:T(8,128)(2,1)} %bitcast.3, bf16[16,160,2,256]{3,2,1,0:T(2,128)(2,1)} %bitcast.4, s32[16]{0:T(128)} %reshape.15.rank_ref, s32[32]{0:T(128)} %ws_ref.1), custom_call_target="tpu_custom_call" | custom-call | tf_op jit(solution)/shard_map/pallas_call | solution.py:433
  138.7 1.6 %copy.7 = bf16[2,256,128]{2,1,0:T(8,128)(2,1)} copy(bf16[2,256,128]{2,1,0:T(8,128)(2,1)} %shard_map.55) | data formatting | bytes 262144

commit v2 on v1

v2 whole, which is shorter than its diff:
```python
import jax
import jax.numpy as jnp
from jax import lax
from jax.experimental import pallas as pl
from jax.experimental.pallas import tpu as pltpu
from jax.sharding import PartitionSpec as P

MESH = pl.DeviceIdType.MESH
BF = jnp.bfloat16
F32 = jnp.float32
NZ, NY, NX = 8, 4, 4
STEPS = 8


def rem(a, b):
    return lax.rem(a, jnp.int32(b))


def div(a, b):
    return lax.div(a, jnp.int32(b))


def kernel(
    field_ref, u_ref, v_ref, rank_ref, ws_ref, out_ref,
    fbuf, gx, zb, mids, oths, osend, relay, fsend, terms, crecv, xs, xr, zsb, zr, fin, fr, fsw, fso,
    uraw, vraw, ut, v2,
    lsem, zss, zrs, yss, yrs, wss, wrs, css, crs, xss, xrs, gss, grs, fss, frs, sss, srs,
):
    src = lax.axis_index("src")
    rcv = lax.axis_index("rcv")
    z, y = div(src, NY), rem(src, NY)
    x, core = div(rcv, 2), rem(rcv, 2)
    own_y, own_e = rem(x, 2) * 2 + core, div(x, 2)
    at_home = own_y == y
    home = jnp.where(at_home, 1, 0).astype(jnp.int32)

    def zdev(offset):
        return (rem(z + (offset + 2 * NZ), NZ) * NY + y, rcv)

    def ydev(offset):
        return (z * NY + rem(y + (offset + NY), NY), rcv)

    sibling = (src, x * 2 + 1 - core)

    def rcopy(source, target, ss, rs, device):
        return pltpu.make_async_remote_copy(
            src_ref=source, dst_ref=target, send_sem=ss, recv_sem=rs,
            device_id=device, device_id_type=MESH,
        )

    load_f = pltpu.make_async_copy(field_ref, fbuf, lsem.at[0])
    load_v = pltpu.make_async_copy(v_ref, vraw, lsem.at[1])
    load_u = pltpu.make_async_copy(u_ref, uraw, lsem.at[2])
    load_f.start()

    barrier = pltpu.get_barrier_semaphore()

    def greet(device):
        pl.semaphore_signal(barrier, inc=1, device_id=device, device_id_type=MESH)

    for offset in (4, 3, 5, 2, 6, 1, 7):
        greet(zdev(offset))
    for offset in range(1, NY):
        greet(ydev(offset))
    greet(sibling)
    for offset in range(1, NX):
        greet((src, rem(x + offset, NX) * 2 + core))

    def last_target(j):
        return (z * NY + own_y, (own_e * 2 + j) * 2 + rem(y, 2))

    def stays(j):
        return jnp.logical_and(at_home, rem(x, 2) == j)

    for j in range(2):
        @pl.when(jnp.logical_not(stays(j)))
        def _():
            greet(last_target(j))

        @pl.when(jnp.logical_not(jnp.logical_and(at_home, div(y, 2) == j)))
        def _():
            greet((z * NY + core + 2 * j, (own_e * 2 + div(y, 2)) * 2 + rem(y, 2)))

    load_f.wait()
    load_v.start()
    load_u.start()
    shift = z + 19 - lax.shift_right_logical(ws_ref[src], jnp.int32(2))

    def roll_block(j, carry):
        block = lax.bitwise_and(shift + j, jnp.int32(7))
        gx[j, :, 0:128] = fbuf[0, block]
        gx[j, :, 128:256] = fbuf[1, block]
        return carry

    lax.fori_loop(0, 10, roll_block, 0)
    pl.semaphore_wait(barrier, 14 + 4 - 2 * home)

    def hop(m):
        return div(m + 1, 2) + jnp.where(m == 6, 1, 0) - jnp.where(m == 7, 1, 0)

    def plus(m):
        return rem(m + jnp.where(m > 5, 1, 0), 2) == 1

    def plane(m):
        h = hop(m)
        return rem(z + 8 + jnp.where(plus(m), -h, h), NZ)

    def forwarded(m):
        return jnp.logical_or(m == 4, m == 7)

    def zcopy(source, chain, kk, direction):
        return rcopy(source, zb.at[chain, kk], zss.at[chain, kk], zrs.at[chain, kk], zdev(direction))

    def ycopy(m, i, mid=None, thin=False):
        toward = ydev(-1) if i in (3, 4, 5, 8, 9) else ydev(1)
        top, low = pl.ds(0, 128), pl.ds(128, 128)
        other = mids if thin else oths
        if i in (0, 3):
            source, target = (mids.at[m, 0] if mid is None else mid), mids.at[m, 3 if i == 0 else 1]
        elif i == 1:
            source, target = osend.at[m, 0], other.at[m, 3]
        elif i == 2:
            source, target = osend.at[m, 2, top], relay.at[m, 0]
        elif i == 4:
            source, target = osend.at[m, 1], other.at[m, 1]
        elif i == 5:
            source, target = osend.at[m, 2, low], relay.at[m, 1]
        elif i == 6:
            source, target = mids.at[m, 3, top], mids.at[m, 2, top]
        elif i == 7:
            source, target = relay.at[m, 0], other.at[m, 2, top]
        elif i == 8:
            source, target = mids.at[m, 1, low], mids.at[m, 2, low]
        else:
            source, target = relay.at[m, 1], other.at[m, 2, low]
        return rcopy(source, target, yss.at[m, i], yrs.at[m, i], toward)

    sides = (0, 1, 3, 2)

    def phase_of(m):
        return lax.bitwise_and(ws_ref[plane(m) * NY + y], jnp.int32(3))

    def ysend(m, mid, upper, lower):
        phase = phase_of(m)

        def rows(i, carry):
            at = pl.ds(pl.multiple_of(i * 32, 32), 32)
            mids[m, 0, at] = mid[at]
            one, two = upper[at], lower[at]
            for k, target in enumerate((oths.at[m, 0], osend.at[m, 0], osend.at[m, 1], osend.at[m, 2])):
                target[at] = jnp.where(rem(y + sides[k], NY) >= phase, one, two)
            return carry

        lax.fori_loop(0, 8, rows, 0)
        for i in (0, 3, 2, 5, 1, 4):
            ycopy(m, i, mid).start()

    def ysend_thin(m, mid, upper, lower):
        phase = phase_of(m)

        def rows(i, carry):
            at = pl.ds(pl.multiple_of(i * 32, 32), 32)
            one, two = mid[at], lower[at]
            oths[m, 0, at] = jnp.where(y >= phase, upper[at], one)
            for k, target in enumerate((mids.at[m, 0], osend.at[m, 0], osend.at[m, 1], osend.at[m, 2])):
                target[at] = jnp.where(rem(y + sides[k], NY) >= phase, one, two)
            return carry

        lax.fori_loop(0, 8, rows, 0)
        for i in (2, 5, 1, 4):
            ycopy(m, i, thin=True).start()

    def yrelay(m):
        @pl.when(jnp.logical_not(forwarded(m)))
        def _():
            for came, onward in ((0, 6), (3, 8), (2, 7), (5, 9)):
                if came in (0, 3):
                    @pl.when(m > 0)
                    def _():
                        ycopy(m, came).wait_recv()
                else:
                    ycopy(m, came).wait_recv()
                ycopy(m, onward).start()

        @pl.when(forwarded(m))
        def _():
            for came, onward in ((2, 7), (5, 9)):
                ycopy(m, came, thin=True).wait_recv()
                ycopy(m, onward, thin=True).start()

    def zneeded(m):
        h = hop(m)

        @pl.when(plus(m))
        def _():
            chain = h - 1
            for i in range(3):
                kk = h - 1 + i
                zcopy(zb.at[chain, kk], chain, kk, 1).wait_recv()
                if i > 0:
                    @pl.when(h < 4)
                    def _():
                        zcopy(zb.at[chain, kk], chain + 1, kk, 1).start()
            ysend(m, zb.at[chain, h], zb.at[chain, h + 1], zb.at[chain, h - 1])

        @pl.when(jnp.logical_not(plus(m)))
        def _():
            chain = h + 3
            for i in range(3):
                kk = 5 - h - i
                zcopy(zb.at[chain, kk], chain, kk, -1).wait_recv()
                if i > 0:
                    @pl.when(h < 3)
                    def _():
                        zcopy(zb.at[chain, kk], chain + 1, kk, -1).start()
            blocks = zb.at[chain, 4 - h], zb.at[chain, 5 - h], zb.at[chain, 3 - h]

            @pl.when(h == 1)
            def _():
                ysend(m, *blocks)

            @pl.when(h > 1)
            def _():
                ysend_thin(m, *blocks)

    def zrest(m):
        h = hop(m)

        @pl.when(plus(m))
        def _():
            def go(kk, carry):
                zcopy(zb.at[h - 1, kk], h - 1, kk, 1).wait_recv()
                zcopy(zb.at[h - 1, kk], h, kk, 1).start()
                return carry

            lax.fori_loop(h + 2, 6, go, 0)

        @pl.when(jnp.logical_not(plus(m)))
        def _():
            def go(i, carry):
                kk = 2 - h - i
                zcopy(zb.at[h + 3, kk], h + 3, kk, -1).wait_recv()
                zcopy(zb.at[h + 3, kk], h + 4, kk, -1).start()
                return carry

            lax.fori_loop(0, 3 - h, go, 0)

    def wcopy(k, late_step):
        if late_step:
            return rcopy(mids.at[4, k], oths.at[7, k], wss.at[1, k - 1], wrs.at[1, k - 1], zdev(-1))
        return rcopy(fsend.at[k - 1], oths.at[4, k], wss.at[0, k - 1], wrs.at[0, k - 1], zdev(-1))

    def mine(k):
        return rem(y + k, 2) == core

    def ccopy(m, k, e):
        j = div(k, 2)
        return rcopy(terms.at[m, k, e], crecv.at[m, j, e], css.at[m, j, e], crs.at[m, j, e], sibling)

    def product(m, k):
        fwd = forwarded(m)

        @pl.when(jnp.logical_and(k == 1, m == 0))
        def _():
            ycopy(m, 3).wait_recv()

        @pl.when(jnp.logical_and(k == 3, m == 0))
        def _():
            ycopy(m, 0).wait_recv()

        @pl.when(k == 1)
        def _():
            ycopy(m, 4).wait_recv()

        @pl.when(k == 3)
        def _():
            ycopy(m, 1).wait_recv()

        @pl.when(k == 2)
        def _():
            ycopy(m, 7).wait_recv()
            ycopy(m, 9).wait_recv()

        @pl.when(jnp.logical_and(k == 2, jnp.logical_not(fwd)))
        def _():
            ycopy(m, 6).wait_recv()
            ycopy(m, 8).wait_recv()

        @pl.when(jnp.logical_and(k > 0, m == 4))
        def _():
            wcopy(k, True).start()
            wcopy(k, False).wait_recv()

        @pl.when(jnp.logical_and(k > 0, m == 7))
        def _():
            wcopy(k, True).wait_recv()

        start = ws_ref[plane(m) * NY + rem(y + k, NY)]
        phase = lax.bitwise_and(start, jnp.int32(3))
        late = jnp.where(y < phase, 1, 0).astype(jnp.int32)
        group = lax.shift_right_logical(start, jnp.int32(2)) + late
        column = lax.bitwise_and(z + 16 - group, jnp.int32(7))
        row = group * 4 + y
        tile0 = lax.shift_right_logical(row, jnp.int32(5)) * 8 + column
        tile1 = lax.shift_right_logical(row + 4, jnp.int32(5)) * 8 + lax.bitwise_and(column + 7, jnp.int32(7))
        swap = jnp.where(fwd, 0, late)

        @pl.when(jnp.logical_and(k > 0, m == 2))
        def _():
            fsend[k - 1] = jnp.where(late == 0, mids[m, k], oths[m, k])

        def item(e, inner):
            tile = jnp.where(e == 0, tile0, tile1)
            block = jnp.where(e + swap == 1, mids[m, k], oths[m, k])
            parts = jnp.dot(v2[tile], block, preferred_element_type=F32)
            w_real = (parts[:160, :128] + parts[160:, 128:]).astype(BF)
            w_imag = (parts[:160, 128:] - parts[160:, :128]).astype(BF)
            stacked = jnp.concatenate(
                [
                    jnp.concatenate([w_real, w_imag], axis=1),
                    jnp.concatenate([-w_imag, w_real], axis=1),
                ],
                axis=0,
            )
            terms[m, k, e] = jnp.dot(ut[tile], stacked, preferred_element_type=F32).astype(BF)
            return inner

        lax.fori_loop(0, 2, item, 0)

        @pl.when(jnp.logical_not(mine(k)))
        def _():
            ccopy(m, k, 0).start()
            ccopy(m, k, 1).start()

        @pl.when(jnp.logical_and(k > 0, m == 2))
        def _():
            wcopy(k, False).start()

    def xcopy(m, k, e):
        j = div(k, 2)
        owner = 2 * e + div(rem(y + k, NY), 2)
        slot = lax.max(rem(x + NX - owner, NX) - 1, jnp.int32(0))
        return rcopy(
            xs.at[m, j, e], xr.at[m, slot], xss.at[m, j, e], xrs.at[m, slot], (src, owner * 2 + core)
        )

    def leaves(k, e):
        return 2 * e + div(rem(y + k, NY), 2) != x

    def core_sum(m, k):
        j = div(k, 2)
        for e in range(2):
            ccopy(m, k, e).wait_recv()
            xs[m, j, e] = (terms[m, k, e].astype(F32) + crecv[m, j, e].astype(F32)).astype(BF)
        for e in range(2):
            @pl.when(leaves(k, e))
            def _():
                xcopy(m, k, e).start()

    def gcopy(m):
        to = jnp.where(m == 6, rem(z + 1, NZ), plane(m))
        return rcopy(zsb.at[m], zr.at[m], gss.at[m], grs.at[m], (to * NY + y, rcv))

    def x_sum(m):
        for j in range(3):
            rcopy(xr.at[m, j], xr.at[m, j], xss.at[m, 0, 0], xrs.at[m, j], sibling).wait_recv()
        total = xs[m, div(rem(own_y + NY - y, NY), 2), own_e].astype(F32)
        for j in range(3):
            total = total + xr[m, j].astype(F32)
        zsb[m] = total.astype(BF)

        @pl.when(m == 7)
        def _():
            gcopy(jnp.int32(6)).wait_recv()
            zsb[m] = (total + zr[6].astype(F32)).astype(BF)

        @pl.when(m > 0)
        def _():
            gcopy(m).start()

    for i in range(6):
        zcopy(gx.at[i + 4], 0, i, 1).start()
        if i < 5:
            zcopy(gx.at[4 - i], 4, 4 - i, -1).start()
    ysend(jnp.int32(0), gx.at[4], gx.at[5], gx.at[3])
    zneeded(jnp.int32(1))
    zneeded(jnp.int32(2))

    load_v.wait()
    load_u.wait()

    def prepare(t, carry):
        keep = lax.broadcasted_iota(jnp.int32, (160, 256), 0) < rank_ref[0, 0, div(t, 8), rem(t, 8)]
        for c in range(2):
            part = vraw[t, :, c, :]
            v2[t, c * 160:(c + 1) * 160, :] = jnp.where(keep, part, jnp.zeros_like(part))
        ut[t] = jnp.transpose(uraw[t])
        return carry

    lax.fori_loop(0, 16, prepare, 0)
    zrest(jnp.int32(1))
    zrest(jnp.int32(2))

    def each(n, action):
        def unit(i, carry):
            k = jnp.where(i < 2, i, jnp.where(i == 2, 3, 2))
            m = jnp.where(i < 3, n, jnp.where(i == 3, n - 1, 0))
            there = jnp.where(i < 3, n < 8, jnp.where(i == 3, n > 1, n == 8))

            @pl.when(there)
            def _():
                action(m, k)

            return carry

        lax.fori_loop(0, 5, unit, 0)

    def summed(m, k):
        @pl.when(mine(k))
        def _():
            core_sum(m, k)

    def step(n, carry):
        @pl.when(jnp.logical_and(n > 0, n < 8))
        def _():
            yrelay(n)

        @pl.when(n == 7)
        def _():
            yrelay(jnp.int32(0))

        @pl.when(jnp.logical_and(n > 0, n < 6))
        def _():
            zneeded(n + 2)

        @pl.when(n > 2)
        def _():
            x_sum(n - 2)

        each(n, product)

        @pl.when(jnp.logical_and(n > 0, n < 4))
        def _():
            zrest(n + 2)

        each(n, summed)
        return carry

    lax.fori_loop(0, STEPS + 1, step, 0)
    x_sum(jnp.int32(7))
    x_sum(jnp.int32(0))

    total = zsb[0].astype(F32)
    for m in (1, 2, 3, 4, 5, 7):
        gcopy(jnp.int32(m)).wait_recv()
        total = total + zr[m].astype(F32)
    fin[...] = total.astype(BF)

    def fcopy(j):
        return rcopy(fin, fr.at[div(y, 2)], fss.at[j], frs.at[div(y, 2)], last_target(j))

    for j in range(2):
        @pl.when(jnp.logical_not(stays(j)))
        def _():
            fcopy(j).start()

        @pl.when(stays(j))
        def _():
            fr[div(y, 2)] = fin[...]

    for j in range(2):
        @pl.when(jnp.logical_not(jnp.logical_and(at_home, div(y, 2) == j)))
        def _():
            rcopy(fin, fr.at[j], fss.at[j], frs.at[j], sibling).wait_recv()

    phase = lax.bitwise_and(ws_ref[src], jnp.int32(3))
    turn = lax.bitwise_and(rem(x, 2) * 2 + lax.bitwise_and(core + phase, jnp.int32(1)) + phase, jnp.int32(3))
    chosen = jnp.where(turn < 2, fr[0], fr[1])
    fsw[...] = chosen
    swapped = rcopy(fsw, fso, sss, srs, sibling)
    swapped.start()
    swapped.wait_recv()
    result = jnp.where(lax.bitwise_and(phase, jnp.int32(1)) == 0, fsw[...], fso[...])
    out_ref[0] = result[:, 0:128]
    out_ref[1] = result[:, 128:256]
    swapped.wait_send()

    for j in range(2):
        @pl.when(jnp.logical_not(stays(j)))
        def _():
            fcopy(j).wait_send()

    for i in range(6):
        zcopy(gx.at[i + 4], 0, i, 1).wait_send()
        if i < 5:
            zcopy(gx.at[4 - i], 4, 4 - i, -1).wait_send()
    for h in range(2, 5):
        for kk in range(h - 1, 6):
            zcopy(zb.at[0, kk], h - 1, kk, 1).wait_send()
    for h in range(2, 4):
        for kk in range(0, 6 - h):
            zcopy(zb.at[0, kk], h + 3, kk, -1).wait_send()
    for k in range(1, 4):
        wcopy(k, False).wait_send()
        wcopy(k, True).wait_send()

    def drain(m, carry):
        @pl.when(jnp.logical_not(forwarded(m)))
        def _():
            for i in range(10):
                ycopy(m, i).wait_send()

        @pl.when(forwarded(m))
        def _():
            for i in (1, 2, 4, 5, 7, 9):
                ycopy(m, i, thin=True).wait_send()

        def inner(k, c):
            for e in range(2):
                @pl.when(jnp.logical_not(mine(k)))
                def _():
                    ccopy(m, k, e).wait_send()

                @pl.when(jnp.logical_and(mine(k), leaves(k, e)))
                def _():
                    xcopy(m, k, e).wait_send()

            return c

        lax.fori_loop(0, 4, inner, 0)

        @pl.when(m > 0)
        def _():
            gcopy(m).wait_send()

        return carry

    lax.fori_loop(0, STEPS, drain, 0)


def body(field, u_basis, v_basis, tile_ranks, window_start):
    fields = field.reshape(2, 8, 256, 128)
    u_tiles = u_basis.reshape(16, 320, 256)
    v_tiles = v_basis.reshape(16, 160, 2, 256)

    def blocks(*lead):
        return pltpu.VMEM((*lead, 256, 256), BF)

    def sems(*shape):
        return pltpu.SemaphoreType.DMA(shape)

    anywhere = pl.BlockSpec(memory_space=pl.ANY)
    scalars = pl.BlockSpec(memory_space=pltpu.SMEM)
    return pl.pallas_call(
        kernel,
        out_shape=jax.ShapeDtypeStruct((2, 256, 128), BF),
        in_specs=[anywhere, anywhere, anywhere, scalars, scalars],
        out_specs=pl.BlockSpec(memory_space=pltpu.VMEM),
        scratch_shapes=[
            pltpu.VMEM((2, 8, 256, 128), BF),
            blocks(10), blocks(7, 6), blocks(8, 4), blocks(8, 4), blocks(8, 3),
            pltpu.VMEM((8, 2, 128, 256), BF),
            blocks(3), blocks(8, 4, 2), blocks(8, 2, 2), blocks(8, 2, 2), blocks(8, 3), blocks(8), blocks(8),
            blocks(), blocks(2), blocks(), blocks(),
            pltpu.VMEM((16, 320, 256), BF),
            pltpu.VMEM((16, 160, 2, 256), BF),
            pltpu.VMEM((16, 256, 320), BF),
            pltpu.VMEM((16, 320, 256), BF),
            sems(3), sems(7, 6), sems(7, 6), sems(8, 10), sems(8, 10), sems(2, 3), sems(2, 3),
            sems(8, 2, 2), sems(8, 2, 2), sems(8, 2, 2), sems(8, 3), sems(8), sems(8), sems(2), sems(2),
            sems(), sems(),
        ],
        compiler_params=pltpu.CompilerParams(
            collective_id=0, has_side_effects=True, vmem_limit_bytes=60 * 1024 * 1024
        ),
    )(fields, u_tiles, v_tiles, tile_ranks, window_start)


def solution(mesh):
    return jax.shard_map(
        body,
        mesh=mesh,
        in_specs=(
            P(None, "rcv", "src"),
            P("src", "rcv", None, None, None, None, None),
            P("src", "rcv", None, None, None, None, None),
            P("src", "rcv", None, None),
            P(),
        ),
        out_specs=P(None, "rcv", "src"),
        check_vma=False,
    )
```

time: 142 us -> 144 us (1.014)
  Pallas kernels: 137 us -> 142 us
    pallas_call x1, Pallas kernels: 137 us -> 142 us  [body(): pl.pallas_call(kernel, out_shape=jax.ShapeDtypeStruct((2, 256, 128), BF),...]
where the time goes in v2:
time: 144 us; the launch traced here: 143 us
  Pallas kernels  142 us (99%)
  local copies, waits for them, and re-layouts  1.57 us (1%)
    pallas_call x1, Pallas kernels, body(): pl.pallas_call(kernel, out_shape=jax.ShapeDtypeStruct((2, 256, 128), BF),...  142 us

profile of v2, /device:TPU:1, one launch (start us, length us, event | category | flops | bytes accessed | tf_op | source)
XLA Modules:
  0.0 143.4 jit_solution(14225766542255462361)
XLA Ops:
  0.0 141.8 %shard_map.55 = bf16[2,256,128]{2,1,0:T(8,128)(2,1)} custom-call(bf16[2,8,256,128]{3,2,1,0:T(8,128)(2,1)} %bitcast.5, bf16[16,320,256]{2,1,0:T(8,128)(2,1)} %bitcast.3, bf16[16,160,2,256]{3,2,1,0:T(2,128)(2,1)} %bitcast.4, s32[1,1,2,8]{3,2,1,0:T(2,128)} %rank_ref.1, s32[32]{0:T(128)} %ws_ref.1), custom_call_target="tpu_custom_call" | custom-call | tf_op jit(solution)/shard_map/pallas_call | solution.py:554
  141.8 1.6 %copy.7 = bf16[2,256,128]{2,1,0:T(8,128)(2,1)} copy(bf16[2,256,128]{2,1,0:T(8,128)(2,1)} %shard_map.55) | data formatting | bytes 262144

commit v3 on v2

--- a/solution.py
+++ b/solution.py
@@ -22,7 +22,7 @@
 
 def kernel(
     field_ref, u_ref, v_ref, rank_ref, ws_ref, out_ref,
-    fbuf, gx, zb, mids, oths, osend, relay, fsend, terms, crecv, xs, xr, zsb, zr, fin, fr, fsw, fso,
+    fbuf, gx, zb, mids, oths, osend, fsend, terms, crecv, xs, xr, zsb, zr, fin, fr, fsw, fso,
     uraw, vraw, ut, v2,
     lsem, zss, zrs, yss, yrs, wss, wrs, css, crs, xss, xrs, gss, grs, fss, frs, sss, srs,
 ):
@@ -112,28 +112,18 @@
         return rcopy(source, zb.at[chain, kk], zss.at[chain, kk], zrs.at[chain, kk], zdev(direction))
 
     def ycopy(m, i, mid=None, thin=False):
-        toward = ydev(-1) if i in (3, 4, 5, 8, 9) else ydev(1)
         top, low = pl.ds(0, 128), pl.ds(128, 128)
         other = mids if thin else oths
-        if i in (0, 3):
-            source, target = (mids.at[m, 0] if mid is None else mid), mids.at[m, 3 if i == 0 else 1]
-        elif i == 1:
-            source, target = osend.at[m, 0], other.at[m, 3]
-        elif i == 2:
-            source, target = osend.at[m, 2, top], relay.at[m, 0]
-        elif i == 4:
-            source, target = osend.at[m, 1], other.at[m, 1]
-        elif i == 5:
-            source, target = osend.at[m, 2, low], relay.at[m, 1]
-        elif i == 6:
-            source, target = mids.at[m, 3, top], mids.at[m, 2, top]
-        elif i == 7:
-            source, target = relay.at[m, 0], other.at[m, 2, top]
-        elif i == 8:
-            source, target = mids.at[m, 1, low], mids.at[m, 2, low]
-        else:
-            source, target = relay.at[m, 1], other.at[m, 2, low]
-        return rcopy(source, target, yss.at[m, i], yrs.at[m, i], toward)
+        source, target, offset = (
+            (mids.at[m, 0] if mid is None else mid, mids.at[m, 3], 1),
+            (mids.at[m, 0] if mid is None else mid, mids.at[m, 1], -1),
+            (osend.at[m, 0], other.at[m, 3], 1),
+            (osend.at[m, 1], other.at[m, 1], -1),
+            (osend.at[m, 2], other.at[m, 2], 2),
+            (mids.at[m, 3, top], mids.at[m, 2, top], 1),
+            (mids.at[m, 1, low], mids.at[m, 2, low], -1),
+        )[i]
+        return rcopy(source, target, yss.at[m, i], yrs.at[m, i], ydev(offset))
 
     sides = (0, 1, 3, 2)
 
@@ -152,7 +142,7 @@
             return carry
 
         lax.fori_loop(0, 8, rows, 0)
-        for i in (0, 3, 2, 5, 1, 4):
+        for i in range(5):
             ycopy(m, i, mid).start()
 
     def ysend_thin(m, mid, upper, lower):
@@ -167,26 +157,18 @@
             return carry
 
         lax.fori_loop(0, 8, rows, 0)
-        for i in (2, 5, 1, 4):
+        for i in (4, 2, 3):
             ycopy(m, i, thin=True).start()
 
     def yrelay(m):
         @pl.when(jnp.logical_not(forwarded(m)))
         def _():
-            for came, onward in ((0, 6), (3, 8), (2, 7), (5, 9)):
-                if came in (0, 3):
-                    @pl.when(m > 0)
-                    def _():
-                        ycopy(m, came).wait_recv()
-                else:
-                    ycopy(m, came).wait_recv()
-                ycopy(m, onward).start()
-
-        @pl.when(forwarded(m))
-        def _():
-            for came, onward in ((2, 7), (5, 9)):
-                ycopy(m, came, thin=True).wait_recv()
-                ycopy(m, onward, thin=True).start()
+            for i in range(2):
+                @pl.when(m > 0)
+                def _():
+                    ycopy(m, i).wait_recv()
+
+                ycopy(m, i + 5).start()
 
     def zneeded(m):
         h = hop(m)
@@ -262,29 +244,28 @@
 
         @pl.when(jnp.logical_and(k == 1, m == 0))
         def _():
+            ycopy(m, 1).wait_recv()
+
+        @pl.when(jnp.logical_and(k == 3, m == 0))
+        def _():
+            ycopy(m, 0).wait_recv()
+
+        @pl.when(k == 1)
+        def _():
             ycopy(m, 3).wait_recv()
 
-        @pl.when(jnp.logical_and(k == 3, m == 0))
-        def _():
-            ycopy(m, 0).wait_recv()
-
-        @pl.when(k == 1)
+        @pl.when(k == 3)
+        def _():
+            ycopy(m, 2).wait_recv()
+
+        @pl.when(k == 2)
         def _():
             ycopy(m, 4).wait_recv()
 
-        @pl.when(k == 3)
-        def _():
-            ycopy(m, 1).wait_recv()
-
-        @pl.when(k == 2)
-        def _():
-            ycopy(m, 7).wait_recv()
-            ycopy(m, 9).wait_recv()
-
         @pl.when(jnp.logical_and(k == 2, jnp.logical_not(fwd)))
         def _():
+            ycopy(m, 5).wait_recv()
             ycopy(m, 6).wait_recv()
-            ycopy(m, 8).wait_recv()
 
         @pl.when(jnp.logical_and(k > 0, m == 4))
         def _():
@@ -433,15 +414,15 @@
         def _():
             zneeded(n + 2)
 
+        each(n, product)
+
+        @pl.when(jnp.logical_and(n > 0, n < 4))
+        def _():
+            zrest(n + 2)
+
         @pl.when(n > 2)
         def _():
             x_sum(n - 2)
-
-        each(n, product)
-
-        @pl.when(jnp.logical_and(n > 0, n < 4))
-        def _():
-            zrest(n + 2)
 
         each(n, summed)
         return carry
@@ -507,12 +488,12 @@
     def drain(m, carry):
         @pl.when(jnp.logical_not(forwarded(m)))
         def _():
-            for i in range(10):
+            for i in range(7):
                 ycopy(m, i).wait_send()
 
         @pl.when(forwarded(m))
         def _():
-            for i in (1, 2, 4, 5, 7, 9):
+            for i in (2, 3, 4):
                 ycopy(m, i, thin=True).wait_send()
 
         def inner(k, c):
@@ -559,14 +540,13 @@
         scratch_shapes=[
             pltpu.VMEM((2, 8, 256, 128), BF),
             blocks(10), blocks(7, 6), blocks(8, 4), blocks(8, 4), blocks(8, 3),
-            pltpu.VMEM((8, 2, 128, 256), BF),
             blocks(3), blocks(8, 4, 2), blocks(8, 2, 2), blocks(8, 2, 2), blocks(8, 3), blocks(8), blocks(8),
             blocks(), blocks(2), blocks(), blocks(),
             pltpu.VMEM((16, 320, 256), BF),
             pltpu.VMEM((16, 160, 2, 256), BF),
             pltpu.VMEM((16, 256, 320), BF),
             pltpu.VMEM((16, 320, 256), BF),
-            sems(3), sems(7, 6), sems(7, 6), sems(8, 10), sems(8, 10), sems(2, 3), sems(2, 3),
+            sems(3), sems(7, 6), sems(7, 6), sems(8, 7), sems(8, 7), sems(2, 3), sems(2, 3),
             sems(8, 2, 2), sems(8, 2, 2), sems(8, 2, 2), sems(8, 3), sems(8), sems(8), sems(2), sems(2),
             sems(), sems(),
         ],

time: 144 us -> 121 us (0.84)
  Pallas kernels: 142 us -> 119 us
    pallas_call x1, Pallas kernels: 142 us -> 119 us  [body(): pl.pallas_call(kernel, out_shape=jax.ShapeDtypeStruct((2, 256, 128), BF),...]
where the time goes in v3:
time: 121 us
  Pallas kernels  119 us (98%)
  local copies, waits for them, and re-layouts  1.57 us (1%)
    pallas_call x1, Pallas kernels, body(): pl.pallas_call(kernel, out_shape=jax.ShapeDtypeStruct((2, 256, 128), BF),...  119 us

profile of v3, /device:TPU:1, one launch (start us, length us, event | category | flops | bytes accessed | tf_op | source)
XLA Modules:
  0.0 121.0 jit_solution(5642980832241528448)
XLA Ops:
  0.0 119.4 %shard_map.55 = bf16[2,256,128]{2,1,0:T(8,128)(2,1)} custom-call(bf16[2,8,256,128]{3,2,1,0:T(8,128)(2,1)} %bitcast.5, bf16[16,320,256]{2,1,0:T(8,128)(2,1)} %bitcast.3, bf16[16,160,2,256]{3,2,1,0:T(2,128)(2,1)} %bitcast.4, s32[1,1,2,8]{3,2,1,0:T(2,128)} %rank_ref.1, s32[32]{0:T(128)} %ws_ref.1), custom_call_target="tpu_custom_call" | custom-call | tf_op jit(solution)/shard_map/pallas_call | solution.py:535
  119.4 1.6 %copy.7 = bf16[2,256,128]{2,1,0:T(8,128)(2,1)} copy(bf16[2,256,128]{2,1,0:T(8,128)(2,1)} %shard_map.55) | data formatting | bytes 262144

commit v4 on v3

--- a/solution.py
+++ b/solution.py
@@ -431,46 +431,6 @@
     x_sum(jnp.int32(7))
     x_sum(jnp.int32(0))
 
-    total = zsb[0].astype(F32)
-    for m in (1, 2, 3, 4, 5, 7):
-        gcopy(jnp.int32(m)).wait_recv()
-        total = total + zr[m].astype(F32)
-    fin[...] = total.astype(BF)
-
-    def fcopy(j):
-        return rcopy(fin, fr.at[div(y, 2)], fss.at[j], frs.at[div(y, 2)], last_target(j))
-
-    for j in range(2):
-        @pl.when(jnp.logical_not(stays(j)))
-        def _():
-            fcopy(j).start()
-
-        @pl.when(stays(j))
-        def _():
-            fr[div(y, 2)] = fin[...]
-
-    for j in range(2):
-        @pl.when(jnp.logical_not(jnp.logical_and(at_home, div(y, 2) == j)))
-        def _():
-            rcopy(fin, fr.at[j], fss.at[j], frs.at[j], sibling).wait_recv()
-
-    phase = lax.bitwise_and(ws_ref[src], jnp.int32(3))
-    turn = lax.bitwise_and(rem(x, 2) * 2 + lax.bitwise_and(core + phase, jnp.int32(1)) + phase, jnp.int32(3))
-    chosen = jnp.where(turn < 2, fr[0], fr[1])
-    fsw[...] = chosen
-    swapped = rcopy(fsw, fso, sss, srs, sibling)
-    swapped.start()
-    swapped.wait_recv()
-    result = jnp.where(lax.bitwise_and(phase, jnp.int32(1)) == 0, fsw[...], fso[...])
-    out_ref[0] = result[:, 0:128]
-    out_ref[1] = result[:, 128:256]
-    swapped.wait_send()
-
-    for j in range(2):
-        @pl.when(jnp.logical_not(stays(j)))
-        def _():
-            fcopy(j).wait_send()
-
     for i in range(6):
         zcopy(gx.at[i + 4], 0, i, 1).wait_send()
         if i < 5:
@@ -510,13 +470,52 @@
 
         lax.fori_loop(0, 4, inner, 0)
 
-        @pl.when(m > 0)
-        def _():
-            gcopy(m).wait_send()
-
         return carry
 
     lax.fori_loop(0, STEPS, drain, 0)
+
+    total = zsb[0].astype(F32)
+    for m in (1, 2, 3, 4, 5, 7):
+        gcopy(jnp.int32(m)).wait_recv()
+        total = total + zr[m].astype(F32)
+    fin[...] = total.astype(BF)
+
+    def fcopy(j):
+        return rcopy(fin, fr.at[div(y, 2)], fss.at[j], frs.at[div(y, 2)], last_target(j))
+
+    for j in range(2):
+        @pl.when(jnp.logical_not(stays(j)))
+        def _():
+            fcopy(j).start()
+
+        @pl.when(stays(j))
+        def _():
+            fr[div(y, 2)] = fin[...]
+
+    for j in range(2):
+        @pl.when(jnp.logical_not(jnp.logical_and(at_home, div(y, 2) == j)))
+        def _():
+            rcopy(fin, fr.at[j], fss.at[j], frs.at[j], sibling).wait_recv()
+
+    phase = lax.bitwise_and(ws_ref[src], jnp.int32(3))
+    turn = lax.bitwise_and(rem(x, 2) * 2 + lax.bitwise_and(core + phase, jnp.int32(1)) + phase, jnp.int32(3))
+    chosen = jnp.where(turn < 2, fr[0], fr[1])
+    fsw[...] = chosen
+    swapped = rcopy(fsw, fso, sss, srs, sibling)
+    swapped.start()
+    swapped.wait_recv()
+    result = jnp.where(lax.bitwise_and(phase, jnp.int32(1)) == 0, fsw[...], fso[...])
+    out_ref[0] = result[:, 0:128]
+    out_ref[1] = result[:, 128:256]
+    swapped.wait_send()
+
+    for j in range(2):
+        @pl.when(jnp.logical_not(stays(j)))
+        def _():
+            fcopy(j).wait_send()
+
+    for m in range(1, STEPS):
+        gcopy(jnp.int32(m)).wait_send()
 
 
 def body(field, u_basis, v_basis, tile_ranks, window_start):

time: 121 us -> 120 us (level)
  no operation moved by 1% of the time
where the time goes in v4:
time: 120 us
  Pallas kernels  119 us (99%)
  local copies, waits for them, and re-layouts  1.57 us (1%)
    pallas_call x1, Pallas kernels, body(): pl.pallas_call(kernel, out_shape=jax.ShapeDtypeStruct((2, 256, 128), BF),...  119 us

profile of v4, /device:TPU:1, one launch (start us, length us, event | category | flops | bytes accessed | tf_op | source)
XLA Modules:
  0.0 120.1 jit_solution(14329247217125460164)
XLA Ops:
  0.0 118.6 %shard_map.55 = bf16[2,256,128]{2,1,0:T(8,128)(2,1)} custom-call(bf16[2,8,256,128]{3,2,1,0:T(8,128)(2,1)} %bitcast.5, bf16[16,320,256]{2,1,0:T(8,128)(2,1)} %bitcast.3, bf16[16,160,2,256]{3,2,1,0:T(2,128)(2,1)} %bitcast.4, s32[1,1,2,8]{3,2,1,0:T(2,128)} %rank_ref.1, s32[32]{0:T(128)} %ws_ref.1), custom_call_target="tpu_custom_call" | custom-call | tf_op jit(solution)/shard_map/pallas_call | solution.py:534
  118.6 1.6 %copy.7 = bf16[2,256,128]{2,1,0:T(8,128)(2,1)} copy(bf16[2,256,128]{2,1,0:T(8,128)(2,1)} %shard_map.55) | data formatting | bytes 262144

commit v5 on v4

--- a/solution.py
+++ b/solution.py
@@ -339,7 +339,7 @@
                 xcopy(m, k, e).start()
 
     def gcopy(m):
-        to = jnp.where(m == 6, rem(z + 1, NZ), plane(m))
+        to = plane(m)
         return rcopy(zsb.at[m], zr.at[m], gss.at[m], grs.at[m], (to * NY + y, rcv))
 
     def x_sum(m):
@@ -349,11 +349,6 @@
         for j in range(3):
             total = total + xr[m, j].astype(F32)
         zsb[m] = total.astype(BF)
-
-        @pl.when(m == 7)
-        def _():
-            gcopy(jnp.int32(6)).wait_recv()
-            zsb[m] = (total + zr[6].astype(F32)).astype(BF)
 
         @pl.when(m > 0)
         def _():
@@ -475,7 +470,7 @@
     lax.fori_loop(0, STEPS, drain, 0)
 
     total = zsb[0].astype(F32)
-    for m in (1, 2, 3, 4, 5, 7):
+    for m in range(1, STEPS):
         gcopy(jnp.int32(m)).wait_recv()
         total = total + zr[m].astype(F32)
     fin[...] = total.astype(BF)

time: 120 us -> 119 us (level)
  no operation moved by 1% of the time
where the time goes in v5:
time: 119 us
  Pallas kernels  118 us (99%)
  local copies, waits for them, and re-layouts  1.57 us (1%)
    pallas_call x1, Pallas kernels, body(): pl.pallas_call(kernel, out_shape=jax.ShapeDtypeStruct((2, 256, 128), BF),...  118 us

profile of v5, /device:TPU:1, one launch (start us, length us, event | category | flops | bytes accessed | tf_op | source)
XLA Modules:
  0.0 119.1 jit_solution(4443017131901290865)
XLA Ops:
  0.0 117.6 %shard_map.55 = bf16[2,256,128]{2,1,0:T(8,128)(2,1)} custom-call(bf16[2,8,256,128]{3,2,1,0:T(8,128)(2,1)} %bitcast.5, bf16[16,320,256]{2,1,0:T(8,128)(2,1)} %bitcast.3, bf16[16,160,2,256]{3,2,1,0:T(2,128)(2,1)} %bitcast.4, s32[1,1,2,8]{3,2,1,0:T(2,128)} %rank_ref.1, s32[32]{0:T(128)} %ws_ref.1), custom_call_target="tpu_custom_call" | custom-call | tf_op jit(solution)/shard_map/pallas_call | solution.py:529
  117.6 1.6 %copy.7 = bf16[2,256,128]{2,1,0:T(8,128)(2,1)} copy(bf16[2,256,128]{2,1,0:T(8,128)(2,1)} %shard_map.55) | data formatting | bytes 262144
